TPU v7x, 32 devices: a whole 2x2x4 slice. The times are simulated.
32 devices in a mesh: dp: 16 (over z, y, x), tensor: 2 (over core).
Axes of the slice: x: 2, y: 2, z: 4, core: 2. Of those that a mesh axis runs over, the one named last changes fastest.
Arguments:
- tokens: bfloat16 [2048, 768], P('dp'), may hold values from -6 to 6
- seq_ids: int32 [2048], P('dp'), may hold values from 0 to 127, as said below
- routes: int32 [2048, 2], P('dp'), may hold values from 0 to 3, all different within a row; in each aligned block of 128 rows (0 to 127, 128 to 255, ...) at most 80 rows name the same one
- gain_attn: float32 [768], replicated, may hold values from 0.25 to 1.75
- w_query: bfloat16 [768, 768], P(None, 'tensor'), may hold values from -0.21875 to 0.21875
- w_key: bfloat16 [768, 768], P(None, 'tensor'), may hold values from -0.21875 to 0.21875
- w_value: bfloat16 [768, 768], P(None, 'tensor'), may hold values from -0.21875 to 0.21875
- w_attn_out: bfloat16 [768, 768], P('tensor'), may hold values from -0.625 to 0.625
- rel_bias: float32 [12, 32], P('tensor'), may hold values from -2.5 to 2.5
- gain_ffn: float32 [768], replicated, may hold values from 0.25 to 1.75
- w_router: bfloat16 [768, 4], replicated, may hold values from -0.145 to 0.145
- expert_in: bfloat16 [16, 768, 768], P('dp', None, 'tensor'), may hold values from -0.21875 to 0.21875
- expert_out: bfloat16 [16, 768, 768], P('dp', 'tensor'), may hold values from -1.75 to 1.75
- cotangent: bfloat16 [2048, 768], P('dp'), may hold values from -6 to 6
Outputs:
- output: bfloat16 [2048, 768], P('dp')
- grad_tokens: float32 [2048, 768], P('dp')
- grad_gain_attn: float32 [768], replicated
- grad_w_query: float32 [768, 768], P(None, 'tensor')
- grad_w_key: float32 [768, 768], P(None, 'tensor')
- grad_w_value: float32 [768, 768], P(None, 'tensor')
- grad_w_attn_out: float32 [768, 768], P('tensor')
- grad_rel_bias: float32 [12, 32], P('tensor')
- grad_gain_ffn: float32 [768], replicated
- grad_w_router: float32 [768, 4], replicated
- grad_expert_in: float32 [16, 768, 768], P('dp', None, 'tensor')
- grad_expert_out: float32 [16, 768, 768], P('dp', 'tensor')
Inputs may be any that keep to these rules, and one draw needn't show every extreme that they name: `seq_ids`: in each device's 128 rows the sequence number starts at 0 and rises by 0 or 1 from row to row; equal numbers form one sequence; in every draw some device holds a single sequence of 128 rows, and some device holds 128 sequences of one row. `routes`: the 2 experts of a row differ; within the 128 rows of one device no expert is named more than 80 times, and in every draw some expert is named exactly 80 times there.
All inputs are finite; a program needn't handle non-finite values.
Results may differ from a plain program's by a relative error of at most 0.017.
Values may be sent and summed in bfloat16 or wider, within the bound.
No kernel may reach another device: no remote copies, remote signals or barrier semaphores. Data moves between devices by JAX's collectives and lax.ppermute only.
A program may use at most 128 MiB of HBM per device.

v0:
```python
import jax
import jax.numpy as jnp
import numpy as np
from jax import lax
from jax.sharding import PartitionSpec as P

HEAD_DIM = 64
TOP = 2
REACH = 64
eps_norm = 1e-06


def bucket_matrix(length, buckets, max_reach):
    exact_span = buckets // 2
    distance = np.arange(length)
    log_ratio = np.log(np.maximum(distance, exact_span) / exact_span) / np.log(
        max_reach / exact_span
    )
    coarse = exact_span + np.floor(log_ratio * (buckets - exact_span)).astype(np.int64)
    bucket_of = np.where(distance < exact_span, distance, np.minimum(coarse, buckets - 1))
    offset = np.maximum(distance[:, None] - distance[None, :], 0)
    return bucket_of[offset].astype(np.int32)


def gelu_tanh(values):
    return jax.nn.gelu(values, approximate=True)


def rms_forward(values, gain_vec):
    inv_rms = lax.rsqrt(jnp.mean(values * values, axis=-1, keepdims=True) + eps_norm)
    return (values * inv_rms * gain_vec, inv_rms)


def rms_backward(grad_normed, values, inv_rms, gain_vec):
    scaled = grad_normed * gain_vec
    inv_cubed = inv_rms * inv_rms * inv_rms
    grad_values = inv_rms * scaled - values * inv_cubed * jnp.mean(
        scaled * values, axis=-1, keepdims=True
    )
    grad_gain = jnp.sum(grad_normed * values * inv_rms, axis=0)
    return (grad_values, grad_gain)


def slot_of(route_ids, experts, capacity):
    count_all = route_ids.shape[0] * route_ids.shape[1]
    flat_ids = route_ids.reshape(-1)
    expert_hot = (flat_ids[:, None] == jnp.arange(experts, dtype=jnp.int32)[None, :]).astype(
        jnp.bfloat16
    )
    order_ids = jnp.arange(count_all, dtype=jnp.int32)
    earlier = (order_ids[:, None] > order_ids[None, :]).astype(jnp.bfloat16)
    before = jnp.dot(earlier, expert_hot, preferred_element_type=jnp.float32)
    rank_in = jnp.sum(before * expert_hot.astype(jnp.float32), axis=1).astype(jnp.int32)
    return (flat_ids * capacity + rank_in).reshape(route_ids.shape)


def head_split(matrix):
    return matrix.reshape(matrix.shape[0], -1, HEAD_DIM)


def attention_scores(queries, key_rows, score_bias, allowed):
    raw_scores = jnp.einsum(
        "qhd,khd->hqk",
        head_split(queries),
        head_split(key_rows),
        preferred_element_type=jnp.float32,
    )
    return jnp.where(allowed[None], raw_scores * HEAD_DIM ** (-0.5) + score_bias, -jnp.inf)


def to_experts(sent_rows, experts, capacity):
    row_width = sent_rows.shape[-1]
    repeated = jnp.broadcast_to(
        sent_rows.reshape(experts, 1, capacity, row_width), (experts, 4, capacity, row_width)
    )
    arrived = lax.all_to_all(
        repeated.reshape(experts * 4, capacity, row_width),
        "dp",
        split_axis=0,
        concat_axis=0,
        tiled=True,
    )
    gathered = arrived.reshape(-1, row_width)
    return gathered


def from_experts(part_rows, experts, capacity):
    row_width = part_rows.shape[-1]
    sources = part_rows.shape[0] // capacity
    returned_rows = lax.all_to_all(
        part_rows.reshape(sources, capacity, row_width),
        "dp",
        split_axis=0,
        concat_axis=0,
        tiled=True,
    )
    summed_rows = jnp.sum(
        returned_rows.reshape(experts, 4, capacity, row_width).astype(jnp.float32), axis=1
    ).reshape(experts * capacity, row_width)
    return summed_rows


def slot_rows(expert_rows, slot_index):
    selected = jnp.take(expert_rows, slot_index, axis=0)
    return selected


def on_device(
    tokens,
    seq_ids,
    routes,
    gain_attn,
    w_query,
    w_key,
    w_value,
    w_attn_out,
    rel_bias,
    gain_ffn,
    w_router,
    expert_in,
    expert_out,
    cotangent,
):
    tok_rows = tokens.shape[0]
    experts = w_router.shape[1]
    bucket_count = rel_bias.shape[1]
    capacity = 4 * ((5 * TOP * tok_rows + 16 * experts - 1) // (16 * experts))
    inputs_wide = tokens.astype(jnp.float32)
    normed_one, inv_one = rms_forward(inputs_wide, gain_attn)
    normed_one = normed_one.astype(jnp.bfloat16)
    queries = jnp.dot(normed_one, w_query, preferred_element_type=jnp.float32).astype(jnp.bfloat16)
    key_rows = jnp.dot(normed_one, w_key, preferred_element_type=jnp.float32).astype(jnp.bfloat16)
    value_rows = jnp.dot(normed_one, w_value, preferred_element_type=jnp.float32).astype(
        jnp.bfloat16
    )
    positions = jnp.arange(tok_rows)
    allowed = (seq_ids[:, None] == seq_ids[None, :]) & (positions[:, None] >= positions[None, :])
    bucket_hot = (
        jnp.asarray(bucket_matrix(tok_rows, bucket_count, REACH))[None]
        == jnp.arange(bucket_count, dtype=jnp.int32)[:, None, None]
    ).astype(jnp.float32)
    score_bias = jnp.einsum("hb,bij->hij", rel_bias, bucket_hot, precision=lax.Precision.HIGHEST)
    scores = attention_scores(queries, key_rows, score_bias, allowed)
    row_max = jnp.max(scores, axis=-1, keepdims=True)
    log_total = row_max + jnp.log(jnp.sum(jnp.exp(scores - row_max), axis=-1, keepdims=True))
    weights = jnp.exp(scores - log_total).astype(jnp.bfloat16)
    mixed_heads = (
        jnp.einsum(
            "hqk,khd->qhd", weights, head_split(value_rows), preferred_element_type=jnp.float32
        )
        .astype(jnp.bfloat16)
        .reshape(tok_rows, -1)
    )
    attended = lax.psum(
        jnp.dot(mixed_heads, w_attn_out, preferred_element_type=jnp.float32), "tensor"
    )
    residual_one = inputs_wide + attended
    normed_two, inv_two = rms_forward(residual_one, gain_ffn)
    normed_two = normed_two.astype(jnp.bfloat16)
    logits = jnp.dot(normed_two, w_router, preferred_element_type=jnp.float32)
    router_max = jnp.max(logits, axis=-1, keepdims=True)
    router_exp = jnp.exp(logits - router_max)
    router_probs = router_exp / jnp.sum(router_exp, axis=-1, keepdims=True)
    route_hot = (routes[:, :, None] == jnp.arange(experts, dtype=jnp.int32)[None, None, :]).astype(
        jnp.float32
    )
    gate_probs = jnp.sum(router_probs[:, None, :] * route_hot, axis=-1)
    slot_index = slot_of(routes, experts, capacity)
    pick_table = (
        slot_index[:, :, None] == jnp.arange(experts * capacity, dtype=jnp.int32)[None, None, :]
    ).astype(jnp.bfloat16)
    dispatched = jnp.einsum(
        "tks,td->sd", pick_table, normed_two, preferred_element_type=jnp.float32
    ).astype(jnp.bfloat16)
    received = to_experts(dispatched, experts, capacity)
    weight_in = expert_in[0]
    weight_out = expert_out[0]
    pre_act = jnp.dot(received, weight_in, preferred_element_type=jnp.float32)
    activated, gelu_back = jax.vjp(gelu_tanh, pre_act)
    activated = activated.astype(jnp.bfloat16)
    expert_part = jnp.dot(activated, weight_out, preferred_element_type=jnp.float32).astype(
        jnp.bfloat16
    )
    expert_rows = from_experts(expert_part, experts, capacity)
    chosen = slot_rows(expert_rows, slot_index)
    grad_wide = cotangent.astype(jnp.float32)
    mixture, grad_gate = lax.psum(
        (
            jnp.sum(gate_probs[:, :, None] * chosen, axis=1),
            jnp.sum(grad_wide[:, None, :] * chosen, axis=-1),
        ),
        "tensor",
    )
    output = (residual_one + mixture).astype(jnp.bfloat16)
    routed_grad = (gate_probs[:, :, None] * grad_wide[:, None, :]).astype(jnp.bfloat16)
    returned = jnp.einsum(
        "tks,tkd->sd", pick_table, routed_grad, preferred_element_type=jnp.float32
    ).astype(jnp.bfloat16)
    grad_rows = to_experts(returned, experts, capacity)
    grad_act = jnp.dot(grad_rows, weight_out.T, preferred_element_type=jnp.float32)
    grad_pre = gelu_back(grad_act)[0].astype(jnp.bfloat16)
    grad_weight_out = jnp.dot(activated.T, grad_rows, preferred_element_type=jnp.float32)
    grad_weight_in = jnp.dot(received.T, grad_pre, preferred_element_type=jnp.float32)
    back_part = jnp.dot(grad_pre, weight_in.T, preferred_element_type=jnp.float32).astype(
        jnp.bfloat16
    )
    back_rows = from_experts(back_part, experts, capacity)
    back_tokens = lax.psum(jnp.sum(slot_rows(back_rows, slot_index), axis=1), "tensor")
    grad_probs = jnp.sum(grad_gate[:, :, None] * route_hot, axis=1)
    grad_logits = (
        router_probs * (grad_probs - jnp.sum(router_probs * grad_probs, axis=-1, keepdims=True))
    ).astype(jnp.bfloat16)
    grad_router = jnp.dot(normed_two.T, grad_logits, preferred_element_type=jnp.float32)
    grad_normed_two = back_tokens + jnp.dot(
        grad_logits, w_router.T, preferred_element_type=jnp.float32
    )
    grad_res_norm, grad_gain_ffn = rms_backward(grad_normed_two, residual_one, inv_two, gain_ffn)
    grad_residual = grad_wide + grad_res_norm
    grad_attended = grad_residual.astype(jnp.bfloat16)
    grad_attn_out = jnp.dot(mixed_heads.T, grad_attended, preferred_element_type=jnp.float32)
    grad_mixed = jnp.dot(grad_attended, w_attn_out.T, preferred_element_type=jnp.float32).astype(
        jnp.bfloat16
    )
    scores_again = attention_scores(queries, key_rows, score_bias, allowed)
    probs_wide = jnp.exp(scores_again - log_total)
    grad_heads = head_split(grad_mixed)
    grad_values = (
        jnp.einsum(
            "hqk,qhd->khd",
            probs_wide.astype(jnp.bfloat16),
            grad_heads,
            preferred_element_type=jnp.float32,
        )
        .astype(jnp.bfloat16)
        .reshape(tok_rows, -1)
    )
    grad_probs_attn = jnp.einsum(
        "qhd,khd->hqk", grad_heads, head_split(value_rows), preferred_element_type=jnp.float32
    )
    delta_rows = jnp.sum(
        grad_heads.astype(jnp.float32) * head_split(mixed_heads).astype(jnp.float32), axis=-1
    ).T[:, :, None]
    grad_scores = probs_wide * (grad_probs_attn - delta_rows)
    grad_bias = jnp.einsum("hij,bij->hb", grad_scores, bucket_hot, precision=lax.Precision.HIGHEST)
    scores_half = grad_scores.astype(jnp.bfloat16)
    score_scale = HEAD_DIM ** (-0.5)
    grad_queries = (
        (
            jnp.einsum(
                "hqk,khd->qhd",
                scores_half,
                head_split(key_rows),
                preferred_element_type=jnp.float32,
            )
            * score_scale
        )
        .astype(jnp.bfloat16)
        .reshape(tok_rows, -1)
    )
    grad_keys = (
        (
            jnp.einsum(
                "hqk,qhd->khd", scores_half, head_split(queries), preferred_element_type=jnp.float32
            )
            * score_scale
        )
        .astype(jnp.bfloat16)
        .reshape(tok_rows, -1)
    )
    grad_query = jnp.dot(normed_one.T, grad_queries, preferred_element_type=jnp.float32)
    grad_key = jnp.dot(normed_one.T, grad_keys, preferred_element_type=jnp.float32)
    grad_value = jnp.dot(normed_one.T, grad_values, preferred_element_type=jnp.float32)
    grad_normed_part = jnp.dot(grad_queries, w_query.T, preferred_element_type=jnp.float32)
    grad_normed_part = grad_normed_part + jnp.dot(
        grad_keys, w_key.T, preferred_element_type=jnp.float32
    )
    grad_normed_part = grad_normed_part + jnp.dot(
        grad_values, w_value.T, preferred_element_type=jnp.float32
    )
    grad_normed_one = lax.psum(grad_normed_part.astype(jnp.bfloat16), "tensor").astype(jnp.float32)
    grad_in_norm, grad_gain_attn = rms_backward(grad_normed_one, inputs_wide, inv_one, gain_attn)
    grad_tokens = grad_residual + grad_in_norm
    summed = lax.psum(
        (
            grad_gain_attn,
            grad_query,
            grad_key,
            grad_value,
            grad_attn_out,
            grad_bias,
            grad_gain_ffn,
            grad_router,
        ),
        "dp",
    )
    return (
        output,
        grad_tokens,
        summed[0],
        summed[1],
        summed[2],
        summed[3],
        summed[4],
        summed[5],
        summed[6],
        summed[7],
        grad_weight_in[None],
        grad_weight_out[None],
    )


def solution(mesh):
    in_specs = (
        P("dp", None),
        P("dp"),
        P("dp", None),
        P(),
        P(None, "tensor"),
        P(None, "tensor"),
        P(None, "tensor"),
        P("tensor", None),
        P("tensor", None),
        P(),
        P(),
        P("dp", None, "tensor"),
        P("dp", "tensor", None),
        P("dp", None),
    )
    out_specs = (
        P("dp", None),
        P("dp", None),
        P(),
        P(None, "tensor"),
        P(None, "tensor"),
        P(None, "tensor"),
        P("tensor", None),
        P("tensor", None),
        P(),
        P(),
        P("dp", None, "tensor"),
        P("dp", "tensor", None),
    )
    return jax.shard_map(
        on_device, mesh=mesh, in_specs=in_specs, out_specs=out_specs, check_vma=False
    )
```

profile of v0, /device:TPU:0, one launch (start us, length us, event | category | flops | bytes accessed | tf_op | source)
XLA Modules:
  0.0 504.1 jit_solution(16210575287183119069)
XLA Ops:
  7.3 1.2 fusion.31
  8.5 0.5 multiply_multiply_fusion.2
  9.0 0.8 fusion.48
  9.8 1.5 convolution_convert_fusion.5
  11.5 1.5 convolution_convert_fusion.4
  13.7 0.7 fusion.1
  15.3 0.6 copy-done.8
  15.9 1.0 fusion.67
  17.7 20.6 %all-reduce.8.cloned.1.call-done = f32[128,768]{1,0:T(8,128)} async-done(((f32[128,768]{1,0:T(8,128)}), f32[128,768]{1,0:T(8,128)}) %all-reduce.8.cloned.1.call-update) | async-done | bytes 393232 | tf_op jit(solution)/shard_map/psum | solution.py:154
  38.3 1.1 multiply_reduce_fusion.4
  39.4 0.5 multiply_multiply_fusion.3
  40.3 1.4 broadcast_in_dim.40
  41.7 7.0 %all-to-all-start = ((bf16[16,80,768]{2,1,0:T(8,128)(2,1)}), bf16[16,80,768]{2,1,0:T(8,128)(2,1)}, u32[]{:S(2)}, u32[]{:S(2)}) async-start(bf16[16,80,768]{2,1,0:T(8,128)(2,1)} %bitcast.8), calls=%async_computation | async-start | bytes 3932160 | tf_op jit(solution)/shard_map/all_to_all | solution.py:76
  49.0 0.4 fusion.9
  49.4 40.4 %all-to-all-done = bf16[16,80,768]{2,1,0:T(8,128)(2,1)} async-done(((bf16[16,80,768]{2,1,0:T(8,128)(2,1)}), bf16[16,80,768]{2,1,0:T(8,128)(2,1)}, u32[]{:S(2)}, u32[]{:S(2)}) %all-to-all-start) | async-done | bytes 1966112 | tf_op jit(solution)/shard_map/all_to_all | solution.py:76
  89.8 1.4 broadcast_in_dim.42
  91.3 9.9 %all-to-all-start.2 = ((bf16[16,80,768]{2,1,0:T(8,128)(2,1)}), bf16[16,80,768]{2,1,0:T(8,128)(2,1)}, u32[]{:S(2)}, u32[]{:S(2)}) async-start(bf16[16,80,768]{2,1,0:T(8,128)(2,1)} %bitcast.17), calls=%async_computation.2 | async-start | bytes 3932160 | tf_op jit(solution)/shard_map/all_to_all | solution.py:76
  101.2 2.7 fusion.26
  103.9 1.3 copy-done.49
  105.2 2.9 convolution_convert_fusion.1
  108.1 33.6 %all-to-all-done.2 = bf16[16,80,768]{2,1,0:T(8,128)(2,1)} async-done(((bf16[16,80,768]{2,1,0:T(8,128)(2,1)}), bf16[16,80,768]{2,1,0:T(8,128)(2,1)}, u32[]{:S(2)}, u32[]{:S(2)}) %all-to-all-start.2) | async-done | bytes 1966112 | tf_op jit(solution)/shard_map/all_to_all | solution.py:76
  141.7 9.2 %all-to-all-start.1 = ((bf16[16,80,768]{2,1,0:T(8,128)(2,1)}), bf16[16,80,768]{2,1,0:T(8,128)(2,1)}, u32[]{:S(2)}, u32[]{:S(2)}) async-start(bf16[16,80,768]{2,1,0:T(8,128)(2,1)} %bitcast.105), calls=%async_computation.1 | async-start | bytes 3932160 | tf_op jit(solution)/shard_map/all_to_all | solution.py:90
  150.9 4.3 fusion.8
  155.2 0.9 copy-done.47
  156.2 2.5 convolution_convert_fusion
  158.6 32.7 %all-to-all-done.1 = bf16[16,80,768]{2,1,0:T(8,128)(2,1)} async-done(((bf16[16,80,768]{2,1,0:T(8,128)(2,1)}), bf16[16,80,768]{2,1,0:T(8,128)(2,1)}, u32[]{:S(2)}, u32[]{:S(2)}) %all-to-all-start.1) | async-done | bytes 1966112 | tf_op jit(solution)/shard_map/all_to_all | solution.py:90
  191.3 8.9 %all-to-all-start.3 = ((bf16[16,80,768]{2,1,0:T(8,128)(2,1)}), bf16[16,80,768]{2,1,0:T(8,128)(2,1)}, u32[]{:S(2)}, u32[]{:S(2)}) async-start(bf16[16,80,768]{2,1,0:T(8,128)(2,1)} %bitcast.104), calls=%async_computation.3 | async-start | bytes 3932160 | tf_op jit(solution)/shard_map/all_to_all | solution.py:90
  200.4 0.7 copy.110
  201.4 1.9 convert_reduce_fusion.1
  203.4 2.0 gather_fusion
  205.3 1.6 reshape.242
  206.9 1.0 multiply_reduce_fusion
  207.9 32.5 %all-to-all-done.3 = bf16[16,80,768]{2,1,0:T(8,128)(2,1)} async-done(((bf16[16,80,768]{2,1,0:T(8,128)(2,1)}), bf16[16,80,768]{2,1,0:T(8,128)(2,1)}, u32[]{:S(2)}, u32[]{:S(2)}) %all-to-all-start.3) | async-done | bytes 1966112 | tf_op jit(solution)/shard_map/all_to_all | solution.py:90
  240.5 1.9 convert_reduce_fusion
  242.4 1.1 gather_fusion.1
  243.5 0.5 reshape.246
  244.1 2.6 select_reduce_fusion
  246.8 2.6 psum.94
  249.4 20.1 %all-reduce.14.cloned.1.call-done = (f32[128,768]{1,0:T(8,128)}, f32[128,768]{1,0:T(8,128)}) async-done(((f32[128,768]{1,0:T(8,128)}, f32[128,768]{1,0:T(8,128)}), (f32[128,768]{1,0:T(8,128)}, f32[128,768]{1,0:T(8,128)})) %all-reduce.14.cloned.1.call-update) | async-done | bytes 786448 | tf_op jit(solution)/shard_map/psum | solution.py:187
  269.6 2.0 multiply_reduce_fusion.2
  271.6 1.7 subtract_add_fusion
  274.1 1.2 fusion.12
  275.3 1.1 fusion.15
  276.5 1.1 fusion.14
  277.6 1.3 fusion.45
  278.9 0.3 fusion.68
  279.2 1.4 fusion.58
  280.7 0.3 convolution_add_fusion.1
  281.0 1.4 fusion.56
  282.5 1.0 fusion.13
  283.6 1.5 fusion.60
  285.1 1.2 copy-done.48
  286.2 3.9 convolution_bitcast_fusion.1
  290.2 3.7 convolution_bitcast_fusion
  294.3 1.1 fusion.16
  295.4 7.5 %all-reduce.10.cloned.1.call-done = bf16[128,768]{1,0:T(8,128)(2,1)} async-done(((bf16[128,768]{1,0:T(8,128)(2,1)}), bf16[128,768]{1,0:T(8,128)(2,1)}) %all-reduce.10.cloned.1.call-update) | async-done | bytes 196624 | tf_op jit(solution)/shard_map/psum | solution.py:280
  302.9 1.1 fusion.37
  304.0 79.7 %all-reduce = (f32[768]{0:T(1024)}, f32[6,32]{1,0:T(8,128)}, f32[768]{0:T(1024)}, f32[768,4]{0,1:T(4,128)}) all-reduce(f32[768]{0:T(1024)S(1)} %get-tuple-element.17, f32[6,32]{1,0:T(8,128)S(1)} %fusion.16, f32[768]{0:T(1024)S(1)} %copy-done.32, f32[768,4]{0,1:T(4,128)S(1)} %fusion.69), channel_id=1, replica_groups=mesh['dp'=16,'tensor'=2] {'dp'}, use_global_device_ids=true, to_apply=%region_25.27 | all-reduce | flops 4800 | bytes 38400 | tf_op jit(solution)/shard_map/psum | solution.py:283
  383.7 1.8 fusion.30
  385.6 106.5 %all-reduce.12.cloned.1.call-done = (f32[768,384]{1,0:T(8,128)}, f32[768,384]{1,0:T(8,128)}, f32[768,384]{1,0:T(8,128)}, f32[384,768]{1,0:T(8,128)}) async-done(((f32[768,384]{1,0:T(8,128)}, f32[768,384]{1,0:T(8,128)}, f32[768,384]{1,0:T(8,128)}, f32[384,768]{1,0:T(8,128)}), (f32[768,384]{1,0:T(8,128)}, f32[768,384]{1,0:T(8,128)}, f32[768,384]{1,0:T(8,128)}, ...) | async-done | bytes 4718608 | tf_op jit(solution)/shard_map/psum | solution.py:283
  492.0 2.5 copy.136
  494.6 1.0 copy.137
  495.6 1.0 copy.138
  496.6 1.0 copy.139
  (144 shorter events, 4.8 us)
Async XLA Ops:
  7.2 98.0 %copy-start = (bf16[1,384,768]{2,1,0:T(8,128)(2,1)S(1)}, bf16[1,384,768]{2,1,0:T(8,128)(2,1)}, u32[]{:S(2)}) copy-start(bf16[1,384,768]{2,1,0:T(8,128)(2,1)} %param.29) | copy-start | bytes 1769476
  7.2 6.5 %copy-start.19 = (s32[128,128]{1,0:T(8,128)S(1)}, s32[128,128]{1,0:T(8,128)}, u32[]{:S(2)}) copy-start(s32[128,128]{1,0:T(8,128)} %constant.43.clone) | copy-start | bytes 196612
  7.2 5.9 %copy-start.1 = (bf16[128,768]{1,0:T(8,128)(2,1)S(1)}, bf16[128,768]{1,0:T(8,128)(2,1)}, u32[]{:S(2)}) copy-start(bf16[128,768]{1,0:T(8,128)(2,1)} %param.17) | copy-start | bytes 589828
  7.2 5.9 %copy-start.18 = (f32[768]{0:T(1024)S(1)}, f32[768]{0:T(1024)}, u32[]{:S(2)}) copy-start(f32[768]{0:T(1024)} %param.20) | copy-start | bytes 9220
  7.2 5.9 %copy-start.2 = (bf16[768,384]{1,0:T(8,128)(2,1)S(1)}, bf16[768,384]{1,0:T(8,128)(2,1)}, u32[]{:S(2)}) copy-start(bf16[768,384]{1,0:T(8,128)(2,1)} %param.23) | copy-start | bytes 1769476
  7.2 6.4 %copy-start.42 = (f32[6,32]{1,0:T(8,128)S(1)}, f32[6,32]{1,0:T(8,128)}, u32[]{:S(2)}) copy-start(f32[6,32]{1,0:T(8,128)} %param.25) | copy-start | bytes 2308
  7.3 31.0 %all-reduce.8.cloned.1.call-start = ((), (), s32[]{:S(2)}) async-start(), calls=%async_computation.4 | async-start | bytes 786432 | tf_op jit(solution)/shard_map/psum | solution.py:154
  9.0 4.1 copy-start.23
  11.5 3.5 copy-start.13
  13.2 1.8 copy-start.14
  13.5 2.4 copy-start.4
  13.7 3.3 copy-start.15
  14.6 2.3 copy-start.33
  14.9 25.0 %copy-start.21 = (f32[768]{0:T(1024)S(1)}, f32[768]{0:T(1024)}, u32[]{:S(2)}) copy-start(f32[768]{0:T(1024)} %param.26) | copy-start | bytes 9220
  15.2 0.7 copy-start.8
  40.0 1.8 copy-start.40
  41.7 7.0 %copy-start.16 = (bf16[128,768]{1,0:T(8,128)(2,1)S(1)}, bf16[128,768]{1,0:T(8,128)(2,1)}, u32[]{:S(2)}) copy-start(bf16[128,768]{1,0:T(8,128)(2,1)} %param.30) | copy-start | bytes 589828
  41.7 7.0 %copy-start.27 = (bf16[768,4]{0,1:T(4,128)(2,1)S(1)}, bf16[768,4]{0,1:T(4,128)(2,1)}, u32[]{:S(2)}) copy-start(bf16[768,4]{0,1:T(4,128)(2,1)} %param.27) | copy-start | bytes 18436
  41.7 48.1 %all-to-all-start = ((bf16[16,80,768]{2,1,0:T(8,128)(2,1)}), bf16[16,80,768]{2,1,0:T(8,128)(2,1)}, u32[]{:S(2)}, u32[]{:S(2)}) async-start(bf16[16,80,768]{2,1,0:T(8,128)(2,1)} %bitcast.8), calls=%async_computation | async-start | bytes 3932160 | tf_op jit(solution)/shard_map/all_to_all | solution.py:76
  48.9 42.4 %copy-start.29 = (f32[128]{0:T(128)}, f32[128]{0:T(128)S(1)}, u32[]{:S(2)}) copy-start(f32[128]{0:T(128)S(1)} %get-tuple-element.41) | copy-start | bytes 1540
  49.0 42.3 %copy-start.35 = (f32[128]{0:T(128)}, f32[128]{0:T(128)S(1)}, u32[]{:S(2)}) copy-start(f32[128]{0:T(128)S(1)} %fusion.55) | copy-start | bytes 1540
  91.2 9.9 %copy-start.46 = (bf16[1,768,384]{2,1,0:T(8,128)(2,1)S(1)}, bf16[1,768,384]{2,1,0:T(8,128)(2,1)}, u32[]{:S(2)}) copy-start(bf16[1,768,384]{2,1,0:T(8,128)(2,1)} %param.28) | copy-start | bytes 1769476
  91.3 50.4 %all-to-all-start.2 = ((bf16[16,80,768]{2,1,0:T(8,128)(2,1)}), bf16[16,80,768]{2,1,0:T(8,128)(2,1)}, u32[]{:S(2)}, u32[]{:S(2)}) async-start(bf16[16,80,768]{2,1,0:T(8,128)(2,1)} %bitcast.17), calls=%async_computation.2 | async-start | bytes 3932160 | tf_op jit(solution)/shard_map/all_to_all | solution.py:76
  103.9 1.3 copy-start.49
  141.7 49.6 %all-to-all-start.1 = ((bf16[16,80,768]{2,1,0:T(8,128)(2,1)}), bf16[16,80,768]{2,1,0:T(8,128)(2,1)}, u32[]{:S(2)}, u32[]{:S(2)}) async-start(bf16[16,80,768]{2,1,0:T(8,128)(2,1)} %bitcast.105), calls=%async_computation.1 | async-start | bytes 3932160 | tf_op jit(solution)/shard_map/all_to_all | solution.py:90
  155.2 0.9 copy-start.47
  191.3 49.1 %all-to-all-start.3 = ((bf16[16,80,768]{2,1,0:T(8,128)(2,1)}), bf16[16,80,768]{2,1,0:T(8,128)(2,1)}, u32[]{:S(2)}, u32[]{:S(2)}) async-start(bf16[16,80,768]{2,1,0:T(8,128)(2,1)} %bitcast.104), calls=%async_computation.3 | async-start | bytes 3932160 | tf_op jit(solution)/shard_map/all_to_all | solution.py:90
  200.2 69.3 %all-reduce.14.cloned.1.call-start = ((), (), s32[]{:S(2)}) async-start(), calls=%async_computation.7 | async-start | bytes 1572864 | tf_op jit(solution)/shard_map/psum | solution.py:187
  244.0 2.8 copy-start.43
  244.0 5.4 %copy-start.34 = (s32[128,2]{0,1:T(2,128)S(1)}, s32[128,2]{0,1:T(2,128)}, u32[]{:S(2)}) copy-start(s32[128,2]{0,1:T(2,128)} %param.19) | copy-start | bytes 3076
  244.0 5.4 %copy-start.30 = (f32[128]{0:T(128)S(1)}, f32[128]{0:T(128)}, u32[]{:S(2)}) copy-start(f32[128]{0:T(128)} %copy-done.29) | copy-start | bytes 1540
  244.0 5.4 %copy-start.36 = (f32[128]{0:T(128)S(1)}, f32[128]{0:T(128)}, u32[]{:S(2)}) copy-start(f32[128]{0:T(128)} %copy-done.35) | copy-start | bytes 1540
  244.0 25.5 %copy-start.22 = (f32[768]{0:T(1024)S(1)}, f32[768]{0:T(1024)}, u32[]{:S(2)}) copy-start(f32[768]{0:T(1024)} %param.26) | copy-start | bytes 9220
  244.0 25.5 %copy-start.28 = (bf16[768,4]{0,1:T(4,128)(2,1)S(1)}, bf16[768,4]{0,1:T(4,128)(2,1)}, u32[]{:S(2)}) copy-start(bf16[768,4]{0,1:T(4,128)(2,1)} %param.27) | copy-start | bytes 18436
  244.0 25.5 %copy-start.41 = (f32[128]{0:T(128)S(1)}, f32[128]{0:T(128)}, u32[]{:S(2)}) copy-start(f32[128]{0:T(128)} %copy-done.40) | copy-start | bytes 1540
  244.0 27.5 %copy-start.17 = (bf16[128,768]{1,0:T(8,128)(2,1)S(1)}, bf16[128,768]{1,0:T(8,128)(2,1)}, u32[]{:S(2)}) copy-start(bf16[128,768]{1,0:T(8,128)(2,1)} %param.30) | copy-start | bytes 589828
  244.1 27.5 %copy-start.45 = (f32[128]{0:T(128)S(1)}, f32[128]{0:T(128)}, u32[]{:S(2)}) copy-start(f32[128]{0:T(128)} %get-tuple-element.37) | copy-start | bytes 1540
  246.7 26.6 %copy-start.5 = (bf16[384,768]{1,0:T(8,128)(2,1)S(1)}, bf16[384,768]{1,0:T(8,128)(2,1)}, u32[]{:S(2)}) copy-start(bf16[384,768]{1,0:T(8,128)(2,1)} %param.24) | copy-start | bytes 1769476
  246.7 56.2 %all-reduce.10.cloned.1.call-start = ((), (), s32[]{:S(2)}) async-start(), calls=%async_computation.5 | async-start | bytes 393216 | tf_op jit(solution)/shard_map/psum | solution.py:280
  249.4 23.9 %copy-start.25 = (f32[128,4]{0,1:T(4,128)}, f32[128,4]{0,1:T(4,128)S(1)}, u32[]{:S(2)}) copy-start(f32[128,4]{0,1:T(4,128)S(1)} %select_reduce_fusion.1) | copy-start | bytes 6148
  249.4 23.9 %copy-start.38 = (f32[128]{0:T(128)}, f32[128]{0:T(128)S(1)}, u32[]{:S(2)}) copy-start(f32[128]{0:T(128)S(1)} %multiply_reduce_fusion.6) | copy-start | bytes 1540
  269.5 4.2 copy-start.9
  274.1 4.8 copy-start.6
  275.3 3.9 copy-start.24
  277.5 3.1 copy-start.7
  279.2 3.3 copy-start.3
  283.5 208.5 %all-reduce.12.cloned.1.call-start = ((), (), s32[]{:S(2)}) async-start(), calls=%async_computation.6 | async-start | bytes 9437184 | tf_op jit(solution)/shard_map/psum | solution.py:283
  285.0 1.2 copy-start.48
  286.2 3.9 copy-start.50
  290.1 3.7 copy-start.26
  290.1 3.7 copy-start.31
  290.1 3.7 copy-start.37
  290.1 3.7 copy-start.39
  290.2 4.2 copy-start.20
  293.9 10.1 %copy-start.32 = (f32[768]{0:T(1024)S(1)}, f32[768]{0:T(1024)}, u32[]{:S(2)}) copy-start(f32[768]{0:T(1024)} %get-tuple-element.15) | copy-start | bytes 9220
  293.9 89.8 %copy-start.44 = (f32[128]{0:T(128)S(1)}, f32[128]{0:T(128)}, u32[]{:S(2)}) copy-start(f32[128]{0:T(128)} %get-tuple-element.35) | copy-start | bytes 1540
  492.0 2.5 copy-start.12
  492.0 3.5 copy-start.11
  494.6 2.0 copy-start.10
Sparse Core Ops, SparseCore 0:
  17.1 21.1 all-reduce.7
  246.8 22.6 all-reduce.13
  283.6 19.2 all-reduce.9
  309.4 182.6 all-reduce.11
where the time goes:
time: 505 us; the launch traced here: 504 us
  waiting for transfers between devices  294 us (58%)
  blocking collectives  82.3 us (16%)
  matrix products  41.1 us (8%)
  starting transfers between devices  35.3 us (7%)
  local copies, waits for them, and re-layouts  20.1 us (4%)
  other arithmetic  16.8 us (3%)
  between operations  14.6 us (3%)
    psum x1, waiting for transfers between devices, on_device(): lax.psum((grad_gain_attn, grad_query, grad_key, grad_value, grad_attn_out...  106 us
    psum x1, blocking collectives, on_device(): lax.psum((grad_gain_attn, grad_query, grad_key, grad_value, grad_attn_out...  79.7 us
    all_to_all x2, waiting for transfers between devices, to_experts(): lax.all_to_all(repeated.reshape(experts * 4, capacity, row_width), 'dp',...  74.1 us
    all_to_all x2, waiting for transfers between devices, from_experts(): lax.all_to_all(part_rows.reshape(sources, capacity, row_width), 'dp', spl...  65.2 us
    psum x1, waiting for transfers between devices, on_device(): lax.psum(jnp.dot(mixed_heads, w_attn_out, preferred_element_type=jnp.floa...  20.6 us
    psum x1, waiting for transfers between devices, on_device(): lax.psum((jnp.sum(gate_probs[:, :, None] * chosen, axis=1), jnp.sum(grad_...  20.1 us
    all_to_all x2, starting transfers between devices, from_experts(): lax.all_to_all(part_rows.reshape(sources, capacity, row_width), 'dp', spl...  18 us
    all_to_all x2, starting transfers between devices, to_experts(): lax.all_to_all(repeated.reshape(experts * 4, capacity, row_width), 'dp',...  16.9 us
  transfers between devices with their start and end apart: 8, of which 8 were waited for; matrix products, arithmetic and copies ran while one was open for 7% of the time, Pallas kernels for 0%

commit v1 on v0

--- a/solution.py
+++ b/solution.py
@@ -151,8 +151,9 @@
         .astype(jnp.bfloat16)
         .reshape(tok_rows, -1)
     )
-    attended = lax.psum(
-        jnp.dot(mixed_heads, w_attn_out, preferred_element_type=jnp.float32), "tensor"
+    update_patches_on = lambda w_in: jnp.sum(lax.all_gather(w_in, "tensor"), axis=0)
+    attended = update_patches_on(
+        jnp.dot(mixed_heads, w_attn_out, preferred_element_type=jnp.float32)
     )
     residual_one = inputs_wide + attended
     normed_two, inv_two = rms_forward(residual_one, gain_ffn)

time: 505 us -> 488 us (0.966)
  waiting for transfers between devices: 294 us -> 275 us
    psum x1 -> x0, waiting for transfers between devices: 20.6 us -> none  [on_device(): lax.psum(jnp.dot(mixed_heads, w_attn_out, preferred_element_type=jnp.floa...]
  transfers between devices with their start and end apart: 8 -> 7, of which waited for: 8 -> 7; matrix products, arithmetic and copies ran while one was open for 7% -> 7% of each run, Pallas kernels for 0% -> 0%
where the time goes in v1:
time: 488 us
  waiting for transfers between devices  275 us (56%)
  blocking collectives  84.6 us (17%)
  matrix products  40.4 us (8%)
  starting transfers between devices  36.4 us (7%)
  local copies, waits for them, and re-layouts  20.5 us (4%)
  other arithmetic  16.5 us (3%)
  between operations  14.5 us (3%)
    psum x1, waiting for transfers between devices, on_device(): lax.psum((grad_gain_attn, grad_query, grad_key, grad_value, grad_attn_out...  108 us
    psum x1, blocking collectives, on_device(): lax.psum((grad_gain_attn, grad_query, grad_key, grad_value, grad_attn_out...  79.6 us
    all_to_all x2, waiting for transfers between devices, to_experts(): lax.all_to_all(repeated.reshape(experts * 4, capacity, row_width), 'dp',...  74 us
    all_to_all x2, waiting for transfers between devices, from_experts(): lax.all_to_all(part_rows.reshape(sources, capacity, row_width), 'dp', spl...  65.2 us
    psum x1, waiting for transfers between devices, on_device(): lax.psum((jnp.sum(gate_probs[:, :, None] * chosen, axis=1), jnp.sum(grad_...  20.1 us
    all_to_all x2, starting transfers between devices, to_experts(): lax.all_to_all(repeated.reshape(experts * 4, capacity, row_width), 'dp',...  18.1 us
    all_to_all x2, starting transfers between devices, from_experts(): lax.all_to_all(part_rows.reshape(sources, capacity, row_width), 'dp', spl...  18 us
    unnamed x107, local copies, waits for them, and re-layouts  10.3 us
  transfers between devices with their start and end apart: 7, of which 7 were waited for; matrix products, arithmetic and copies ran while one was open for 7% of the time, Pallas kernels for 0%

profile of v1, /device:TPU:0, one launch (start us, length us, event | category | flops | bytes accessed | tf_op | source)
XLA Modules:
  0.0 487.5 jit_solution(14146158456611691396)
XLA Ops:
  7.3 1.1 fusion.31
  8.4 0.5 multiply_multiply_fusion.2
  8.9 0.8 fusion.48
  9.7 0.8 copy.106
  11.1 0.7 compare_and_fusion
  11.9 1.5 convolution_convert_fusion.5
  13.5 1.5 convolution_convert_fusion.4
  15.2 0.3 convolution_convert_fusion.6
  15.7 0.7 fusion.1
  17.9 2.4 all-gather
  20.5 0.5 multiply_multiply_fusion.3
  21.4 1.4 broadcast_in_dim.40
  22.8 8.4 %all-to-all-start = ((bf16[16,80,768]{2,1,0:T(8,128)(2,1)}), bf16[16,80,768]{2,1,0:T(8,128)(2,1)}, u32[]{:S(2)}, u32[]{:S(2)}) async-start(bf16[16,80,768]{2,1,0:T(8,128)(2,1)} %bitcast.9), calls=%async_computation | async-start | bytes 3932160 | tf_op jit(solution)/shard_map/all_to_all | solution.py:76
  31.6 0.4 fusion.9
  32.0 40.5 %all-to-all-done = bf16[16,80,768]{2,1,0:T(8,128)(2,1)} async-done(((bf16[16,80,768]{2,1,0:T(8,128)(2,1)}), bf16[16,80,768]{2,1,0:T(8,128)(2,1)}, u32[]{:S(2)}, u32[]{:S(2)}) %all-to-all-start) | async-done | bytes 1966112 | tf_op jit(solution)/shard_map/all_to_all | solution.py:76
  72.5 1.4 broadcast_in_dim.42
  73.9 9.6 %all-to-all-start.2 = ((bf16[16,80,768]{2,1,0:T(8,128)(2,1)}), bf16[16,80,768]{2,1,0:T(8,128)(2,1)}, u32[]{:S(2)}, u32[]{:S(2)}) async-start(bf16[16,80,768]{2,1,0:T(8,128)(2,1)} %bitcast.18), calls=%async_computation.2 | async-start | bytes 3932160 | tf_op jit(solution)/shard_map/all_to_all | solution.py:76
  83.5 2.7 fusion.26
  86.3 1.3 copy-done.49
  87.6 2.9 convolution_convert_fusion.1
  90.4 33.5 %all-to-all-done.2 = bf16[16,80,768]{2,1,0:T(8,128)(2,1)} async-done(((bf16[16,80,768]{2,1,0:T(8,128)(2,1)}), bf16[16,80,768]{2,1,0:T(8,128)(2,1)}, u32[]{:S(2)}, u32[]{:S(2)}) %all-to-all-start.2) | async-done | bytes 1966112 | tf_op jit(solution)/shard_map/all_to_all | solution.py:76
  124.0 9.2 %all-to-all-start.1 = ((bf16[16,80,768]{2,1,0:T(8,128)(2,1)}), bf16[16,80,768]{2,1,0:T(8,128)(2,1)}, u32[]{:S(2)}, u32[]{:S(2)}) async-start(bf16[16,80,768]{2,1,0:T(8,128)(2,1)} %bitcast.107), calls=%async_computation.1 | async-start | bytes 3932160 | tf_op jit(solution)/shard_map/all_to_all | solution.py:90
  133.1 4.3 fusion.8
  137.5 0.9 copy-done.47
  138.4 2.5 convolution_convert_fusion
  140.9 32.7 %all-to-all-done.1 = bf16[16,80,768]{2,1,0:T(8,128)(2,1)} async-done(((bf16[16,80,768]{2,1,0:T(8,128)(2,1)}), bf16[16,80,768]{2,1,0:T(8,128)(2,1)}, u32[]{:S(2)}, u32[]{:S(2)}) %all-to-all-start.1) | async-done | bytes 1966112 | tf_op jit(solution)/shard_map/all_to_all | solution.py:90
  173.6 8.9 %all-to-all-start.3 = ((bf16[16,80,768]{2,1,0:T(8,128)(2,1)}), bf16[16,80,768]{2,1,0:T(8,128)(2,1)}, u32[]{:S(2)}, u32[]{:S(2)}) async-start(bf16[16,80,768]{2,1,0:T(8,128)(2,1)} %bitcast.106), calls=%async_computation.3 | async-start | bytes 3932160 | tf_op jit(solution)/shard_map/all_to_all | solution.py:90
  182.7 0.7 copy.110
  183.7 1.9 convert_reduce_fusion.1
  185.6 2.0 gather_fusion
  187.6 1.6 reshape.243
  189.2 1.0 multiply_reduce_fusion
  190.2 32.5 %all-to-all-done.3 = bf16[16,80,768]{2,1,0:T(8,128)(2,1)} async-done(((bf16[16,80,768]{2,1,0:T(8,128)(2,1)}), bf16[16,80,768]{2,1,0:T(8,128)(2,1)}, u32[]{:S(2)}, u32[]{:S(2)}) %all-to-all-start.3) | async-done | bytes 1966112 | tf_op jit(solution)/shard_map/all_to_all | solution.py:90
  222.7 1.9 convert_reduce_fusion
  224.7 1.1 gather_fusion.1
  225.7 0.5 reshape.247
  226.3 2.6 select_reduce_fusion
  229.0 2.6 psum.86
  231.7 20.1 %all-reduce.11.cloned.1.call-done = (f32[128,768]{1,0:T(8,128)}, f32[128,768]{1,0:T(8,128)}) async-done(((f32[128,768]{1,0:T(8,128)}, f32[128,768]{1,0:T(8,128)}), (f32[128,768]{1,0:T(8,128)}, f32[128,768]{1,0:T(8,128)})) %all-reduce.11.cloned.1.call-update) | async-done | bytes 786448 | tf_op jit(solution)/shard_map/psum | solution.py:188
  251.8 2.0 multiply_reduce_fusion.2
  253.8 1.7 subtract_add_fusion
  256.3 1.2 fusion.12
  257.6 1.1 fusion.15
  258.7 1.1 fusion.14
  259.8 1.3 fusion.45
  261.1 0.3 fusion.68
  261.5 1.5 fusion.58
  262.9 0.3 convolution_add_fusion.1
  263.3 1.4 fusion.56
  264.7 1.0 fusion.13
  265.8 1.4 fusion.60
  267.3 1.2 copy-done.48
  268.5 3.9 convolution_bitcast_fusion.1
  272.4 3.7 convolution_bitcast_fusion
  276.6 1.1 fusion.16
  277.6 7.5 %all-reduce.7.cloned.1.call-done = bf16[128,768]{1,0:T(8,128)(2,1)} async-done(((bf16[128,768]{1,0:T(8,128)(2,1)}), bf16[128,768]{1,0:T(8,128)(2,1)}) %all-reduce.7.cloned.1.call-update) | async-done | bytes 196624 | tf_op jit(solution)/shard_map/psum | solution.py:281
  285.2 1.1 fusion.37
  286.3 79.6 %all-reduce = (f32[768]{0:T(1024)}, f32[6,32]{1,0:T(8,128)}, f32[768]{0:T(1024)}, f32[768,4]{0,1:T(4,128)}) all-reduce(f32[768]{0:T(1024)S(1)} %get-tuple-element.17, f32[6,32]{1,0:T(8,128)S(1)} %fusion.16, f32[768]{0:T(1024)S(1)} %copy-done.32, f32[768,4]{0,1:T(4,128)S(1)} %fusion.69), channel_id=1, replica_groups=mesh['dp'=16,'tensor'=2] {'dp'}, use_global_device_ids=true, to_apply=%region_25.27 | all-reduce | flops 4800 | bytes 38400 | tf_op jit(solution)/shard_map/psum | solution.py:284
  365.9 1.8 fusion.30
  367.7 107.7 %all-reduce.9.cloned.1.call-done = (f32[768,384]{1,0:T(8,128)}, f32[768,384]{1,0:T(8,128)}, f32[768,384]{1,0:T(8,128)}, f32[384,768]{1,0:T(8,128)}) async-done(((f32[768,384]{1,0:T(8,128)}, f32[768,384]{1,0:T(8,128)}, f32[768,384]{1,0:T(8,128)}, f32[384,768]{1,0:T(8,128)}), (f32[768,384]{1,0:T(8,128)}, f32[768,384]{1,0:T(8,128)}, f32[768,384]{1,0:T(8,128)}, ...) | async-done | bytes 4718608 | tf_op jit(solution)/shard_map/psum | solution.py:284
  475.4 2.5 copy.135
  477.9 1.0 copy.136
  479.0 1.0 copy.137
  480.0 1.0 copy.138
  (143 shorter events, 5.1 us)
Async XLA Ops:
  7.2 80.4 %copy-start = (bf16[1,384,768]{2,1,0:T(8,128)(2,1)S(1)}, bf16[1,384,768]{2,1,0:T(8,128)(2,1)}, u32[]{:S(2)}) copy-start(bf16[1,384,768]{2,1,0:T(8,128)(2,1)} %param.29) | copy-start | bytes 1769476
  7.2 8.5 %copy-start.19 = (s32[128,128]{1,0:T(8,128)S(1)}, s32[128,128]{1,0:T(8,128)}, u32[]{:S(2)}) copy-start(s32[128,128]{1,0:T(8,128)} %constant.43.clone) | copy-start | bytes 196612
  7.2 8.0 %copy-start.1 = (bf16[128,768]{1,0:T(8,128)(2,1)S(1)}, bf16[128,768]{1,0:T(8,128)(2,1)}, u32[]{:S(2)}) copy-start(bf16[128,768]{1,0:T(8,128)(2,1)} %param.17) | copy-start | bytes 589828
  7.2 8.0 %copy-start.18 = (f32[768]{0:T(1024)S(1)}, f32[768]{0:T(1024)}, u32[]{:S(2)}) copy-start(f32[768]{0:T(1024)} %param.20) | copy-start | bytes 9220
  7.2 8.0 %copy-start.2 = (bf16[768,384]{1,0:T(8,128)(2,1)S(1)}, bf16[768,384]{1,0:T(8,128)(2,1)}, u32[]{:S(2)}) copy-start(bf16[768,384]{1,0:T(8,128)(2,1)} %param.23) | copy-start | bytes 1769476
  7.2 8.4 %copy-start.42 = (f32[6,32]{1,0:T(8,128)S(1)}, f32[6,32]{1,0:T(8,128)}, u32[]{:S(2)}) copy-start(f32[6,32]{1,0:T(8,128)} %param.25) | copy-start | bytes 2308
  8.9 7.5 %copy-start.23 = (f32[128]{0:T(128)}, f32[128]{0:T(128)S(1)}, u32[]{:S(2)}) copy-start(f32[128]{0:T(128)S(1)} %get-tuple-element.36) | copy-start | bytes 1540
  13.5 3.4 copy-start.13
  15.2 1.8 copy-start.14
  15.5 1.7 copy-start.4
  15.7 1.9 copy-start.15
  17.2 0.6 copy-start.8
  17.3 3.8 copy-start.21
  21.0 1.8 copy-start.40
  22.8 8.5 %copy-start.16 = (bf16[128,768]{1,0:T(8,128)(2,1)S(1)}, bf16[128,768]{1,0:T(8,128)(2,1)}, u32[]{:S(2)}) copy-start(bf16[128,768]{1,0:T(8,128)(2,1)} %param.30) | copy-start | bytes 589828
  22.8 8.5 %copy-start.27 = (bf16[768,4]{0,1:T(4,128)(2,1)S(1)}, bf16[768,4]{0,1:T(4,128)(2,1)}, u32[]{:S(2)}) copy-start(bf16[768,4]{0,1:T(4,128)(2,1)} %param.27) | copy-start | bytes 18436
  22.8 8.8 %copy-start.33 = (s32[128,2]{0,1:T(2,128)S(1)}, s32[128,2]{0,1:T(2,128)}, u32[]{:S(2)}) copy-start(s32[128,2]{0,1:T(2,128)} %param.19) | copy-start | bytes 3076
  22.8 49.6 %all-to-all-start = ((bf16[16,80,768]{2,1,0:T(8,128)(2,1)}), bf16[16,80,768]{2,1,0:T(8,128)(2,1)}, u32[]{:S(2)}, u32[]{:S(2)}) async-start(bf16[16,80,768]{2,1,0:T(8,128)(2,1)} %bitcast.9), calls=%async_computation | async-start | bytes 3932160 | tf_op jit(solution)/shard_map/all_to_all | solution.py:76
  31.5 42.4 %copy-start.29 = (f32[128]{0:T(128)}, f32[128]{0:T(128)S(1)}, u32[]{:S(2)}) copy-start(f32[128]{0:T(128)S(1)} %get-tuple-element.41) | copy-start | bytes 1540
  31.5 42.3 %copy-start.35 = (f32[128]{0:T(128)}, f32[128]{0:T(128)S(1)}, u32[]{:S(2)}) copy-start(f32[128]{0:T(128)S(1)} %fusion.55) | copy-start | bytes 1540
  73.9 9.7 %copy-start.46 = (bf16[1,768,384]{2,1,0:T(8,128)(2,1)S(1)}, bf16[1,768,384]{2,1,0:T(8,128)(2,1)}, u32[]{:S(2)}) copy-start(bf16[1,768,384]{2,1,0:T(8,128)(2,1)} %param.28) | copy-start | bytes 1769476
  73.9 50.1 %all-to-all-start.2 = ((bf16[16,80,768]{2,1,0:T(8,128)(2,1)}), bf16[16,80,768]{2,1,0:T(8,128)(2,1)}, u32[]{:S(2)}, u32[]{:S(2)}) async-start(bf16[16,80,768]{2,1,0:T(8,128)(2,1)} %bitcast.18), calls=%async_computation.2 | async-start | bytes 3932160 | tf_op jit(solution)/shard_map/all_to_all | solution.py:76
  86.3 1.3 copy-start.49
  124.0 49.6 %all-to-all-start.1 = ((bf16[16,80,768]{2,1,0:T(8,128)(2,1)}), bf16[16,80,768]{2,1,0:T(8,128)(2,1)}, u32[]{:S(2)}, u32[]{:S(2)}) async-start(bf16[16,80,768]{2,1,0:T(8,128)(2,1)} %bitcast.107), calls=%async_computation.1 | async-start | bytes 3932160 | tf_op jit(solution)/shard_map/all_to_all | solution.py:90
  137.5 0.9 copy-start.47
  173.6 49.1 %all-to-all-start.3 = ((bf16[16,80,768]{2,1,0:T(8,128)(2,1)}), bf16[16,80,768]{2,1,0:T(8,128)(2,1)}, u32[]{:S(2)}, u32[]{:S(2)}) async-start(bf16[16,80,768]{2,1,0:T(8,128)(2,1)} %bitcast.106), calls=%async_computation.3 | async-start | bytes 3932160 | tf_op jit(solution)/shard_map/all_to_all | solution.py:90
  182.5 69.3 %all-reduce.11.cloned.1.call-start = ((), (), s32[]{:S(2)}) async-start(), calls=%async_computation.6 | async-start | bytes 1572864 | tf_op jit(solution)/shard_map/psum | solution.py:188
  226.2 2.8 copy-start.43
  226.2 5.4 %copy-start.34 = (s32[128,2]{0,1:T(2,128)S(1)}, s32[128,2]{0,1:T(2,128)}, u32[]{:S(2)}) copy-start(s32[128,2]{0,1:T(2,128)} %param.19) | copy-start | bytes 3076
  226.2 5.4 %copy-start.30 = (f32[128]{0:T(128)S(1)}, f32[128]{0:T(128)}, u32[]{:S(2)}) copy-start(f32[128]{0:T(128)} %copy-done.29) | copy-start | bytes 1540
  226.3 5.4 %copy-start.36 = (f32[128]{0:T(128)S(1)}, f32[128]{0:T(128)}, u32[]{:S(2)}) copy-start(f32[128]{0:T(128)} %copy-done.35) | copy-start | bytes 1540
  226.3 25.5 %copy-start.22 = (f32[768]{0:T(1024)S(1)}, f32[768]{0:T(1024)}, u32[]{:S(2)}) copy-start(f32[768]{0:T(1024)} %param.26) | copy-start | bytes 9220
  226.3 25.5 %copy-start.28 = (bf16[768,4]{0,1:T(4,128)(2,1)S(1)}, bf16[768,4]{0,1:T(4,128)(2,1)}, u32[]{:S(2)}) copy-start(bf16[768,4]{0,1:T(4,128)(2,1)} %param.27) | copy-start | bytes 18436
  226.3 25.5 %copy-start.41 = (f32[128]{0:T(128)S(1)}, f32[128]{0:T(128)}, u32[]{:S(2)}) copy-start(f32[128]{0:T(128)} %copy-done.40) | copy-start | bytes 1540
  226.3 27.5 %copy-start.17 = (bf16[128,768]{1,0:T(8,128)(2,1)S(1)}, bf16[128,768]{1,0:T(8,128)(2,1)}, u32[]{:S(2)}) copy-start(bf16[128,768]{1,0:T(8,128)(2,1)} %param.30) | copy-start | bytes 589828
  226.3 27.5 %copy-start.45 = (f32[128]{0:T(128)S(1)}, f32[128]{0:T(128)}, u32[]{:S(2)}) copy-start(f32[128]{0:T(128)} %get-tuple-element.37) | copy-start | bytes 1540
  228.9 26.6 %copy-start.5 = (bf16[384,768]{1,0:T(8,128)(2,1)S(1)}, bf16[384,768]{1,0:T(8,128)(2,1)}, u32[]{:S(2)}) copy-start(bf16[384,768]{1,0:T(8,128)(2,1)} %param.24) | copy-start | bytes 1769476
  229.0 56.2 %all-reduce.7.cloned.1.call-start = ((), (), s32[]{:S(2)}) async-start(), calls=%async_computation.4 | async-start | bytes 393216 | tf_op jit(solution)/shard_map/psum | solution.py:281
  231.7 23.9 %copy-start.25 = (f32[128,4]{0,1:T(4,128)}, f32[128,4]{0,1:T(4,128)S(1)}, u32[]{:S(2)}) copy-start(f32[128,4]{0,1:T(4,128)S(1)} %select_reduce_fusion.1) | copy-start | bytes 6148
  231.7 23.9 %copy-start.38 = (f32[128]{0:T(128)}, f32[128]{0:T(128)S(1)}, u32[]{:S(2)}) copy-start(f32[128]{0:T(128)S(1)} %multiply_reduce_fusion.6) | copy-start | bytes 1540
  251.8 4.2 copy-start.9
  256.3 4.8 copy-start.6
  257.6 3.9 copy-start.24
  259.8 3.1 copy-start.7
  261.5 3.3 copy-start.3
  265.8 209.6 %all-reduce.9.cloned.1.call-start = ((), (), s32[]{:S(2)}) async-start(), calls=%async_computation.5 | async-start | bytes 9437184 | tf_op jit(solution)/shard_map/psum | solution.py:284
  267.3 1.2 copy-start.48
  268.5 3.9 copy-start.50
  272.4 3.7 copy-start.26
  272.4 3.7 copy-start.31
  272.4 3.7 copy-start.37
  272.4 3.7 copy-start.39
  272.4 4.2 copy-start.20
  276.1 10.1 %copy-start.32 = (f32[768]{0:T(1024)S(1)}, f32[768]{0:T(1024)}, u32[]{:S(2)}) copy-start(f32[768]{0:T(1024)} %get-tuple-element.15) | copy-start | bytes 9220
  276.2 89.7 %copy-start.44 = (f32[128]{0:T(128)S(1)}, f32[128]{0:T(128)}, u32[]{:S(2)}) copy-start(f32[128]{0:T(128)} %get-tuple-element.35) | copy-start | bytes 1540
  475.4 2.5 copy-start.12
  475.4 3.5 copy-start.11
  477.9 2.0 copy-start.10
Sparse Core Ops, SparseCore 0:
  229.1 22.6 all-reduce.10
  265.9 19.2 all-reduce.6
  292.8 182.5 all-reduce.8
